TPU v7x, 256 devices: a whole 4x4x8 slice. The times are simulated.
256 devices in a mesh: wide: 32 (over z, y_lo, core), narrow: 8 (over x, y_hi).
Axes of the slice: x: 4, y: 4 (y_hi: 2, y_lo: 2; y = y_hi * 2 + y_lo), z: 8, core: 2. Of those that a mesh axis runs over, the one named last changes fastest.
Arguments:
- gradient: bfloat16 [40960, 16384], P(('wide', 'narrow')), may hold values from -81 to 81
- seating: int32 [64], replicated, may hold values from 0 to 63, each once
Outputs:
- rotated: bfloat16 [40960, 16384], P(('wide', 'narrow'))
Inputs may be any that keep to these rules, and one draw needn't show every extreme that they name: `seating`: each of the 64 block numbers is the seat of exactly one block.
All inputs are finite; a program needn't handle non-finite values.
Results may differ from a plain program's by a relative error of at most 0.0075.
Values may be sent and summed in bfloat16 or wider, within the bound.
A program may use at most 64 MiB of HBM per device.

v0:
```python
import jax
import jax.numpy as jnp
from jax import lax
from jax.sharding import PartitionSpec as P

ROUNDS = 8
STEPS = 2


def advance(seat_of, total_slots):
    pair_count = total_slots // 2
    cycle_pos = jnp.where(seat_of % 2 == 0, seat_of // 2 - 1, total_slots - 2 - (seat_of - 1) // 2)
    next_pos = (cycle_pos + 1) % (total_slots - 1)
    new_slot = jnp.where(
        next_pos < pair_count - 1, 2 * (next_pos + 1), 2 * (total_slots - 2 - next_pos) + 1
    )
    return jnp.where(seat_of == 0, 0, new_slot)


def occupants(seat_of, total_slots):
    block_ids = jnp.arange(total_slots, dtype=jnp.int32)
    matches = seat_of[None, :] == block_ids[:, None]
    return jnp.sum(jnp.where(matches, block_ids[None, :], 0), axis=1)


def rotate_columns(matrix, cosine, sine_part):
    width = cosine.shape[0]
    left_cols = matrix[:, :width]
    right_cols = matrix[:, width:]
    return jnp.concatenate(
        [left_cols * cosine - right_cols * sine_part, left_cols * sine_part + right_cols * cosine],
        axis=1,
    )


def roll_second(matrix, offset, which_axis):
    head_part, tail_part = jnp.split(matrix, 2, axis=which_axis)
    return jnp.concatenate(
        [head_part, jnp.roll(tail_part, offset, axis=which_axis)], axis=which_axis
    )


def one_round(round_index, carried):
    gram_mat, rotation = carried
    width = gram_mat.shape[0] // 2
    left_diag = jnp.diagonal(gram_mat[:width, :width])
    right_diag = jnp.diagonal(gram_mat[width:, width:])
    off_diag = jnp.diagonal(gram_mat[:width, width:])
    spread = right_diag - left_diag
    damping = (left_diag + right_diag) / 16.0 + 1e-06
    radius = jnp.sqrt(spread * spread + 4.0 * off_diag * off_diag + damping * damping)
    tangent = 2.0 * off_diag / (spread + radius)
    cosine = 1.0 / jnp.sqrt(1.0 + tangent * tangent)
    sine_part = tangent * cosine
    gram_mat = rotate_columns(gram_mat, cosine, sine_part)
    gram_mat = rotate_columns(gram_mat.T, cosine, sine_part).T
    rotation = rotate_columns(rotation, cosine, sine_part)
    gram_mat = roll_second(roll_second(gram_mat, -1, 0), -1, 1)
    rotation = roll_second(rotation, -1, 1)
    return (gram_mat, rotation)


def rotations(gram_mat):
    initial = (gram_mat, jnp.eye(gram_mat.shape[0], dtype=jnp.float32))
    gram_mat, rotation = lax.fori_loop(0, ROUNDS, one_round, initial)
    return roll_second(rotation, ROUNDS, 1)


def update_pair(paired):
    contract_dims = (((0,), (0,)), ((), ()))
    partial_gram = lax.dot_general(
        paired, paired, contract_dims, preferred_element_type=jnp.float32
    )
    gram_mat = lax.psum(partial_gram, "narrow")
    rotation = rotations(gram_mat).astype(jnp.bfloat16)
    return jnp.dot(paired, rotation, preferred_element_type=jnp.float32).astype(jnp.bfloat16)


def per_device(gradient, seating):
    count_wide = lax.axis_size("wide")
    row_count = gradient.shape[0]
    total_slots = 2 * count_wide
    block_width = gradient.shape[1] // total_slots
    seat_of = seating
    holders = occupants(seat_of, total_slots)
    seated = jnp.take(gradient.reshape(row_count, total_slots, block_width), holders, axis=1)
    seated = seated.reshape(row_count, count_wide, 2, block_width)
    arrived = lax.all_to_all(seated, "wide", split_axis=1, concat_axis=0, tiled=True)
    paired = arrived.reshape(count_wide * row_count, 2 * block_width)
    for section_index in range(STEPS):
        paired = update_pair(paired)
        if section_index + 1 < STEPS:
            following = advance(seat_of, total_slots)
            returned = lax.all_to_all(
                paired.reshape(count_wide * row_count, 1, 2, block_width),
                "wide",
                split_axis=0,
                concat_axis=1,
                tiled=True,
            )
            slotted = returned.reshape(row_count, total_slots, block_width)
            source_slots = jnp.take(seat_of, occupants(following, total_slots))
            regrouped = jnp.take(slotted, source_slots, axis=1).reshape(
                row_count, count_wide, 2, block_width
            )
            arrived = lax.all_to_all(regrouped, "wide", split_axis=1, concat_axis=0, tiled=True)
            paired = arrived.reshape(count_wide * row_count, 2 * block_width)
            seat_of = following
    returned = lax.all_to_all(
        paired.reshape(count_wide * row_count, 1, 2, block_width),
        "wide",
        split_axis=0,
        concat_axis=1,
        tiled=True,
    )
    slotted = returned.reshape(row_count, total_slots, block_width)
    return jnp.take(slotted, seat_of, axis=1).reshape(row_count, total_slots * block_width)


def solution(mesh):
    in_specs = (P(("wide", "narrow"), None), P())
    out_specs = P(("wide", "narrow"), None)
    return jax.shard_map(
        per_device, mesh=mesh, in_specs=in_specs, out_specs=out_specs, check_vma=False
    )
```

profile of v0, /device:TPU:1, one launch (start us, length us, event | category | flops | bytes accessed | tf_op | source)
XLA Modules:
  0.0 1019.4 jit_solution(16833773583891870454)
XLA Ops:
  7.3 5.5 copy.84
  12.9 5.7 gather_fusion.7
  18.6 5.4 broadcast_select_fusion.1
  23.9 10.2 copy.68
  34.1 129.0 %all_to_all.60 = bf16[160,32,2,256]{3,2,0,1:T(2,128)(2,1)S(1)} all-to-all(bf16[160,32,2,256]{3,2,0,1:T(2,128)(2,1)} %copy.68), channel_id=1, replica_groups=mesh['wide'=32,'narrow'=8] {'wide'}, dimensions={1} | all-to-all | bytes 10485760 | tf_op jit(solution)/shard_map/all_to_all | solution.py:88
  164.0 2.3 copy-done.3
  166.3 3.9 fusion.32
  171.4 85.2 %all-reduce.3.cloned.1.call-done = f32[512,512]{1,0:T(8,128)} async-done(((f32[512,512]{1,0:T(8,128)}), f32[512,512]{1,0:T(8,128)}) %all-reduce.3.cloned.1.call-update) | async-done | bytes 1048592 | tf_op jit(solution)/shard_map/psum | solution.py:74
  256.6 103.8 %while.24 = (s32[]{:T(128)}, f32[512,512]{1,0:T(8,128)}, f32[512,512]{0,1:T(8,128)}, s32[]{:T(128)}) while((s32[]{:T(128)}, f32[512,512]{1,0:T(8,128)}, f32[512,512]{0,1:T(8,128)}, s32[]{:T(128)}) %tuple.72), condition=%wide.region_3.5_spmd, body=%wide.region_2.4_spmd.sunk | while | flops 6034946 | bytes 28854352 | solution.py:65
  257.9 2.3 gather_fusion
  260.2 2.3 gather_fusion.1
  262.6 2.3 gather_fusion.2
  270.8 2.3 gather_fusion
  273.2 2.3 gather_fusion.1
  275.5 2.3 gather_fusion.2
  283.8 2.3 gather_fusion
  286.1 2.3 gather_fusion.1
  288.5 2.3 gather_fusion.2
  296.8 2.3 gather_fusion
  299.1 2.3 gather_fusion.1
  301.5 2.3 gather_fusion.2
  309.7 2.3 gather_fusion
  312.1 2.3 gather_fusion.1
  314.4 2.3 gather_fusion.2
  322.7 2.3 gather_fusion
  361.7 7.6 convolution_convert_fusion.1
  369.3 13.6 %copy.69 = bf16[5120,1,2,256]{3,2,1,0:T(2,128)(2,1)} copy(bf16[5120,1,2,256]{0,3,2,1:T(8,128)(2,1)} %bitcast.90) | data formatting | bytes 10485760 | tf_op jit(solution)/shard_map/reshape | solution.py:95
  382.9 12.9 %all-to-all-start.1 = ((bf16[5120,1,2,256]{3,2,1,0:T(2,128)(2,1)}), bf16[5120,1,2,256]{3,2,1,0:T(2,128)(2,1)}, u32[]{:S(2)}, u32[]{:S(2)}) async-start(bf16[5120,1,2,256]{3,2,1,0:T(2,128)(2,1)} %copy.69), calls=%async_computation.1 | async-start | bytes 10485760 | tf_op jit(solution)/shard_map/all_to_all | solution.py:94
  397.1 117.8 %all-to-all-done.1 = bf16[5120,1,2,256]{3,2,1,0:T(2,128)(2,1)} async-done(((bf16[5120,1,2,256]{3,2,1,0:T(2,128)(2,1)}), bf16[5120,1,2,256]{3,2,1,0:T(2,128)(2,1)}, u32[]{:S(2)}, u32[]{:S(2)}) %all-to-all-start.1) | async-done | bytes 5242912 | tf_op jit(solution)/shard_map/all_to_all | solution.py:94
  514.9 3.2 copy.70
  518.0 2.8 copy.71
  520.9 5.7 gather_fusion.8
  526.5 5.4 broadcast_select_fusion
  531.9 10.2 copy.72
  542.1 121.9 %all_to_all.61 = bf16[160,32,2,256]{3,2,0,1:T(2,128)(2,1)S(1)} all-to-all(bf16[160,32,2,256]{3,2,0,1:T(2,128)(2,1)} %copy.72), channel_id=1, replica_groups=mesh['wide'=32,'narrow'=8] {'wide'}, dimensions={1} | all-to-all | bytes 10485760 | tf_op jit(solution)/shard_map/all_to_all | solution.py:106
  664.9 2.3 copy-done.4
  667.2 3.9 fusion.33
  671.1 84.2 %all-reduce.5.cloned.1.call-done = f32[512,512]{1,0:T(8,128)} async-done(((f32[512,512]{1,0:T(8,128)}), f32[512,512]{1,0:T(8,128)}) %all-reduce.5.cloned.1.call-update) | async-done | bytes 1048592 | tf_op jit(solution)/shard_map/psum | solution.py:74
  755.3 86.5 %while.25 = (s32[]{:T(128)}, f32[512,512]{1,0:T(8,128)}, f32[512,512]{0,1:T(8,128)S(1)}, s32[]{:T(128)}) while((s32[]{:T(128)}, f32[512,512]{1,0:T(8,128)}, f32[512,512]{0,1:T(8,128)S(1)}, s32[]{:T(128)}) %tuple.75), condition=%wide.region_7.9_spmd, body=%wide.region_6.8_spmd.sunk | while | flops 6034946 | bytes 28854352 | solution.py:65
  842.0 7.6 convolution_convert_fusion
  849.5 13.6 %copy.73 = bf16[5120,1,2,256]{3,2,1,0:T(2,128)(2,1)} copy(bf16[5120,1,2,256]{0,3,2,1:T(8,128)(2,1)} %bitcast.91) | data formatting | bytes 10485760 | tf_op jit(solution)/shard_map/reshape | solution.py:110
  863.1 12.8 %all-to-all-start.3 = ((bf16[5120,1,2,256]{3,2,1,0:T(2,128)(2,1)}), bf16[5120,1,2,256]{3,2,1,0:T(2,128)(2,1)}, u32[]{:S(2)}, u32[]{:S(2)}) async-start(bf16[5120,1,2,256]{3,2,1,0:T(2,128)(2,1)} %copy.73), calls=%async_computation.3 | async-start | bytes 10485760 | tf_op jit(solution)/shard_map/all_to_all | solution.py:109
  875.9 119.0 %all-to-all-done.3 = bf16[5120,1,2,256]{3,2,1,0:T(2,128)(2,1)} async-done(((bf16[5120,1,2,256]{3,2,1,0:T(2,128)(2,1)}), bf16[5120,1,2,256]{3,2,1,0:T(2,128)(2,1)}, u32[]{:S(2)}, u32[]{:S(2)}) %all-to-all-start.3) | async-done | bytes 5242912 | tf_op jit(solution)/shard_map/all_to_all | solution.py:109
  995.0 3.2 copy.74
  998.2 2.8 copy.75
  1001.0 5.7 gather_fusion.9
  1006.6 3.0 select_bitcast_fusion
  1009.7 2.9 copy.80
  (369 shorter events, 157.0 us)
Async XLA Ops:
  6.5 250.1 %all-reduce.3.cloned.1.call-start = ((), (), s32[]{:S(2)}) async-start(), calls=%async_computation.4 | async-start | bytes 2097152 | tf_op jit(solution)/shard_map/psum | solution.py:74
  164.0 2.4 copy-start.3
  256.6 8.4 copy-start.1
  269.6 8.4 copy-start.1
  282.5 8.4 copy-start.1
  295.5 8.4 copy-start.1
  308.5 8.4 copy-start.1
  321.4 8.4 copy-start.1
  334.4 8.4 copy-start.1
  347.4 8.4 copy-start.1
  382.9 13.2 %copy-start = (s32[64]{0:T(128)S(1)}, s32[64]{0:T(128)}, u32[]{:S(2)}) copy-start(s32[64]{0:T(128)} %param.9) | copy-start | bytes 772
  382.9 132.0 %all-to-all-start.1 = ((bf16[5120,1,2,256]{3,2,1,0:T(2,128)(2,1)}), bf16[5120,1,2,256]{3,2,1,0:T(2,128)(2,1)}, u32[]{:S(2)}, u32[]{:S(2)}) async-start(bf16[5120,1,2,256]{3,2,1,0:T(2,128)(2,1)} %copy.69), calls=%async_computation.1 | async-start | bytes 10485760 | tf_op jit(solution)/shard_map/all_to_all | solution.py:94
  395.8 359.5 %all-reduce.5.cloned.1.call-start = ((), (), s32[]{:S(2)}) async-start(), calls=%async_computation.5 | async-start | bytes 2097152 | tf_op jit(solution)/shard_map/psum | solution.py:74
  664.9 2.4 copy-start.4
  755.3 8.4 copy-start.2
  766.1 8.4 copy-start.2
  776.9 8.4 copy-start.2
  787.7 8.4 copy-start.2
  798.6 8.4 copy-start.2
  809.4 8.4 copy-start.2
  820.2 8.4 copy-start.2
  831.0 8.4 copy-start.2
  863.1 131.8 %all-to-all-start.3 = ((bf16[5120,1,2,256]{3,2,1,0:T(2,128)(2,1)}), bf16[5120,1,2,256]{3,2,1,0:T(2,128)(2,1)}, u32[]{:S(2)}, u32[]{:S(2)}) async-start(bf16[5120,1,2,256]{3,2,1,0:T(2,128)(2,1)} %copy.73), calls=%async_computation.3 | async-start | bytes 10485760 | tf_op jit(solution)/shard_map/all_to_all | solution.py:109
Sparse Core Ops, SparseCore 0:
  170.4 86.1 all-reduce.2
  671.3 83.9 all-reduce.4
where the time goes:
time: 1020 us
  waiting for transfers between devices  406 us (40%)
  blocking collectives  251 us (25%)
  local copies, waits for them, and re-layouts  232 us (23%)
  other arithmetic  65.9 us (6%)
  starting transfers between devices  25.9 us (3%)
  matrix products  22.9 us (2%)
  between operations  13.6 us (1%)
    all_to_all x2, waiting for transfers between devices, per_device(): lax.all_to_all(paired.reshape(count_wide * row_count, 1, 2, block_width),...  237 us
    psum x2, waiting for transfers between devices, update_pair(): gram_mat = lax.psum(partial_gram, 'narrow')  169 us
    all_to_all x1, blocking collectives, per_device(): lax.all_to_all(seated, 'wide', split_axis=1, concat_axis=0, tiled=True)  129 us
    all_to_all x1, blocking collectives, per_device(): lax.all_to_all(regrouped, 'wide', split_axis=1, concat_axis=0, tiled=True)  122 us
    gather x16, local copies, waits for them, and re-layouts, one_round(): off_diag = jnp.diagonal(gram_mat[:width, width:])  37.5 us
    gather x16, local copies, waits for them, and re-layouts, one_round(): right_diag = jnp.diagonal(gram_mat[width:, width:])  37.5 us
    gather x16, local copies, waits for them, and re-layouts, one_round(): left_diag = jnp.diagonal(gram_mat[:width, :width])  37.5 us
    reshape x2, local copies, waits for them, and re-layouts, per_device(): paired.reshape(count_wide * row_count, 1, 2, block_width)  27.2 us
  transfers between devices with their start and end apart: 4, of which 4 were waited for; matrix products, arithmetic and copies ran while one was open for 0% of the time, Pallas kernels for 0%

commit v1 on v0

v1 whole, which is shorter than its diff:
```python
import functools

import jax
import jax.numpy as jnp
from jax import lax
from jax.experimental import pallas as pl
from jax.experimental.pallas import tpu as pltpu
from jax.sharding import PartitionSpec as P

ROUNDS = 8
BW = 256
F32 = jnp.float32
BF16 = jnp.bfloat16


def advance(seat_of, total_slots):
    pair_count = total_slots // 2
    cycle_pos = jnp.where(seat_of % 2 == 0, seat_of // 2 - 1, total_slots - 2 - (seat_of - 1) // 2)
    next_pos = (cycle_pos + 1) % (total_slots - 1)
    new_slot = jnp.where(
        next_pos < pair_count - 1, 2 * (next_pos + 1), 2 * (total_slots - 2 - next_pos) + 1
    )
    return jnp.where(seat_of == 0, 0, new_slot)


def occupants(seat_of, total_slots):
    block_ids = jnp.arange(total_slots, dtype=jnp.int32)
    matches = seat_of[None, :] == block_ids[:, None]
    return jnp.sum(jnp.where(matches, block_ids[None, :], 0), axis=1).astype(jnp.int32)


def init_masks(mask_ref):
    s = lax.broadcasted_iota(jnp.int32, (8, 128), 0)
    c = lax.broadcasted_iota(jnp.int32, (8, 128), 1)
    for t in range(-1, 17):
        d = 8 * t + s - c
        mask_ref[t + 1] = jnp.where((d >= -7) & (d <= 7), 1.0, 0.0).astype(F32)
    for t in range(17):
        d = 8 * t + s - c
        mask_ref[18 + t] = jnp.where((d >= 0) & (d <= 7), 1.0, 0.0).astype(F32)


def dot_t(a, b):
    return lax.dot_general(a, b, (((0,), (0,)), ((), ())), preferred_element_type=F32)


def gram_band(left, right, mask_ref, g_ref, store):
    g_ref[0] = dot_t(left, right)
    g_ref[1] = dot_t(left, left)
    g_ref[2] = dot_t(right, right)
    for j in range(2):
        lanes = slice(128 * j, 128 * j + 128)
        acc = [jnp.zeros((8, 128), F32) for _ in range(4)]
        for t in range(-1, 17):
            u = (16 * j + t) % 32
            acc[u % 2] += g_ref[0, 8 * u : 8 * u + 8, lanes] * mask_ref[t + 1]
        for t in range(17):
            u = (16 * j + t) % 32
            mask = mask_ref[18 + t]
            acc[2 + u % 2] += g_ref[1, 8 * u : 8 * u + 8, lanes] * mask
            acc[2 + (u + 1) % 2] += g_ref[2, 8 * u : 8 * u + 8, lanes] * mask
        for r in range(4):
            store(slice(8 * r, 8 * r + 8), lanes, acc[r])


def lane_roll(x, back):
    return pltpu.roll(x, (-back) % x.shape[1], 1)


def row_roll(x, down):
    return pltpu.roll(x, down % x.shape[0], 0)


def iota(shape, axis):
    return lax.broadcasted_iota(jnp.int32, shape, axis)


def skew(x, sign):
    c = iota(x.shape, 1)
    for b in (1, 2, 4, 8):
        x = jnp.where((c & b) != 0, row_roll(x, sign * b), x)
    return x


def spread(x):
    y = jnp.broadcast_to(x, (8, x.shape[1]))
    d = iota(y.shape, 0)
    for b in (1, 2, 4):
        y = jnp.where((d & b) != 0, lane_roll(y, b), y)
    return y


def rotation_band(band):
    cross = skew(band[:16], -1)
    own = skew(band[16:], -1)
    lr = cross[:8]
    ll = own[:8]
    rr = own[8:]
    d = iota((8, BW), 0)
    flipped = [lr[0:1]] + [lane_roll(cross[16 - k : 17 - k], k) for k in range(1, 8)]
    rl = jnp.concatenate(flipped, axis=0)
    ca = jnp.where(d == 0, 1.0, 0.0).astype(F32)
    cb = jnp.zeros((8, BW), F32)
    cc = jnp.zeros((8, BW), F32)
    cd = ca
    for r in range(ROUNDS):
        a = ll[0:1]
        c = rr[0:1]
        off = lr[0:1]
        spread_ac = c - a
        damp = (a + c) / 16.0 + 1e-06
        radius = jnp.sqrt(spread_ac * spread_ac + 4.0 * off * off + damp * damp)
        tangent = 2.0 * off / (spread_ac + radius)
        cs = 1.0 / jnp.sqrt(1.0 + tangent * tangent)
        sn = tangent * cs
        if r < ROUNDS - 1:
            csd = spread(cs)
            snd = spread(sn)
            ll1 = ll * cs - lr * sn
            lr1 = ll * sn + lr * cs
            rl1 = rl * cs - rr * sn
            rr1 = rl * sn + rr * cs
            ll = csd * ll1 - snd * rl1
            rl = snd * ll1 + csd * rl1
            lr = csd * lr1 - snd * rr1
            rr = snd * lr1 + csd * rr1
        ca, cc = cs * ca - sn * cc, sn * ca + cs * cc
        cb, cd = cs * cb - sn * cd, sn * cb + cs * cd
        if r < ROUNDS - 1:
            lr = jnp.where(d == 0, row_roll(rl, -1), row_roll(lane_roll(lr, 1), 1))
            rl = jnp.where(d == 7, 0.0, row_roll(rl, -1))
            rr = lane_roll(rr, 1)
            cc = jnp.where(d == 0, 0.0, row_roll(lane_roll(cc, 1), 1))
            cd = jnp.where(d == 0, 0.0, row_roll(lane_roll(cd, 1), 1))
    first = jnp.concatenate([ca, cb], axis=0)
    second = row_roll(jnp.concatenate([lane_roll(cd, -7), lane_roll(cc, -7)], axis=0), 1)
    return jnp.concatenate([skew(first, 1), skew(second, 1)], axis=0)


def build_dense(rot, m_ref):
    wide = rot.astype(F32)
    s = iota((16, 128), 0)
    c = iota((16, 128), 1)
    for half in range(2):
        part = wide[16 * half : 16 * half + 16]
        turned = jnp.concatenate([part[8:], part[:8]], axis=0)
        for j in range(2):
            lanes = slice(128 * j, 128 * j + 128)
            out_lanes = slice(256 * half + 128 * j, 256 * half + 128 * j + 128)
            for g in (range(0, 9) if half == 0 else range(-1, 8)):
                d = 16 * g + s - c
                keep = ((d >= 0) & (d <= 7)) if half == 0 else ((d >= -7) & (d <= 0))
                row = 16 * ((g + 8 * j) % 16)
                m_ref[row : row + 16, out_lanes] = jnp.where(keep, part[:, lanes], 0.0).astype(BF16)
                m_ref[256 + row : 256 + row + 16, out_lanes] = jnp.where(
                    keep, turned[:, lanes], 0.0
                ).astype(BF16)


def apply_dense(left, right, m_ref):
    new = jnp.dot(left, m_ref[:256], preferred_element_type=F32)
    return (new + jnp.dot(right, m_ref[256:], preferred_element_type=F32)).astype(BF16)


def gram_kernel(hold, l_ref, r_ref, out_ref, mask_ref, g_ref):
    @pl.when(pl.program_id(0) == 0)
    def _():
        init_masks(mask_ref)

    def store(rows, lanes, value):
        out_ref[0, rows, lanes] = value

    gram_band(l_ref[...], r_ref[...], mask_ref, g_ref, store)


def previous_seats(q, pairs):
    left = jnp.where(q == 0, 0, jnp.where(q == 1, 1, 2 * q - 2))
    right = jnp.where(q == pairs - 1, 2 * pairs - 2, 2 * q + 3)
    return left, right


def middle_kernel(pairs, hold, l_ref, r_ref, rot_ref, x_ref, out_ref, mask_ref, g_ref, m_ref):
    p = pl.program_id(0)

    @pl.when(p == 0)
    def _():
        init_masks(mask_ref)
        m_ref[...] = jnp.zeros_like(m_ref)

    @pl.when(p < pairs)
    def _():
        build_dense(rot_ref[0], m_ref)
        cols = pl.ds(pl.multiple_of(p * 2 * BW, 2 * BW), 2 * BW)
        x_ref[:, cols] = apply_dense(l_ref[...], r_ref[...], m_ref)

    @pl.when(p >= 1)
    def _():
        def store(rows, lanes, value):
            out_ref[0, rows, lanes] = value

        left, right = previous_seats(p - 1, pairs)
        l_new = x_ref[:, pl.ds(pl.multiple_of(left * BW, BW), BW)]
        r_new = x_ref[:, pl.ds(pl.multiple_of(right * BW, BW), BW)]
        gram_band(l_new, r_new, mask_ref, g_ref, store)


def last_kernel(pairs, hold, l_ref, r_ref, rot_ref, out_ref, m_ref, y_ref):
    q = pl.program_id(0)
    side = pl.program_id(1)

    @pl.when((q == 0) & (side == 0))
    def _():
        m_ref[...] = jnp.zeros_like(m_ref)

    @pl.when(side == 0)
    def _():
        build_dense(rot_ref[0], m_ref)
        new = apply_dense(l_ref[...], r_ref[...], m_ref)
        out_ref[...] = new[:, :BW]
        y_ref[...] = new[:, BW:]

    @pl.when(side == 1)
    def _():
        out_ref[...] = y_ref[...]


def gram_call(x, holders, pairs):
    rows = x.shape[0]
    return pl.pallas_call(
        gram_kernel,
        out_shape=jax.ShapeDtypeStruct((pairs, 32, BW), F32),
        grid_spec=pltpu.PrefetchScalarGridSpec(
            num_scalar_prefetch=1,
            grid=(pairs,),
            in_specs=[
                pl.BlockSpec((rows, BW), lambda p, h: (0, h[2 * p])),
                pl.BlockSpec((rows, BW), lambda p, h: (0, h[2 * p + 1])),
            ],
            out_specs=pl.BlockSpec((1, 32, BW), lambda p, h: (p, 0, 0)),
            scratch_shapes=[pltpu.VMEM((35, 8, 128), F32), pltpu.VMEM((3, BW, BW), F32)],
        ),
    )(holders, x, x)


def middle_call(x, holders, rot, pairs):
    rows, cols = x.shape
    last = pairs - 1
    return pl.pallas_call(
        functools.partial(middle_kernel, pairs),
        out_shape=(
            jax.ShapeDtypeStruct((rows, cols), BF16),
            jax.ShapeDtypeStruct((pairs, 32, BW), F32),
        ),
        grid_spec=pltpu.PrefetchScalarGridSpec(
            num_scalar_prefetch=1,
            grid=(pairs + 1,),
            in_specs=[
                pl.BlockSpec((rows, BW), lambda p, h: (0, h[2 * jnp.minimum(p, last)])),
                pl.BlockSpec((rows, BW), lambda p, h: (0, h[2 * jnp.minimum(p, last) + 1])),
                pl.BlockSpec((1, 32, BW), lambda p, h: (jnp.minimum(p, last), 0, 0)),
            ],
            out_specs=(
                pl.BlockSpec((rows, cols), lambda p, h: (0, 0)),
                pl.BlockSpec((1, 32, BW), lambda p, h: (jnp.maximum(p - 1, 0), 0, 0)),
            ),
            scratch_shapes=[
                pltpu.VMEM((35, 8, 128), F32),
                pltpu.VMEM((3, BW, BW), F32),
                pltpu.VMEM((2 * BW, 2 * BW), BF16),
            ],
        ),
    )(holders, x, x, rot)


def last_call(x, holders, rot, pairs):
    rows, cols = x.shape
    return pl.pallas_call(
        functools.partial(last_kernel, pairs),
        out_shape=jax.ShapeDtypeStruct((rows, cols), BF16),
        grid_spec=pltpu.PrefetchScalarGridSpec(
            num_scalar_prefetch=1,
            grid=(pairs, 2),
            in_specs=[
                pl.BlockSpec((rows, BW), lambda q, s, h: (0, previous_seats(q, pairs)[0])),
                pl.BlockSpec((rows, BW), lambda q, s, h: (0, previous_seats(q, pairs)[1])),
                pl.BlockSpec((1, 32, BW), lambda q, s, h: (q, 0, 0)),
            ],
            out_specs=pl.BlockSpec((rows, BW), lambda q, s, h: (0, h[2 * q + s])),
            scratch_shapes=[pltpu.VMEM((2 * BW, 2 * BW), BF16), pltpu.VMEM((rows, BW), BF16)],
        ),
    )(holders, x, x, rot)


def rounds_call(band):
    def kernel(in_ref, out_ref):
        out_ref[...] = rotation_band(in_ref[...]).astype(BF16)

    return pl.pallas_call(kernel, out_shape=jax.ShapeDtypeStruct((32, BW), BF16))(band)


def exchange(band, pairs):
    total = lax.psum(band, ("wide", "narrow"))
    mine = lax.dynamic_index_in_dim(total, lax.axis_index("wide"), 0, keepdims=False)
    return lax.all_gather(rounds_call(mine), "wide", axis=0, tiled=False)


def per_device(gradient, seating):
    slots = gradient.shape[1] // BW
    pairs = slots // 2
    seat_of = seating.astype(jnp.int32)
    first = occupants(seat_of, slots)
    second = occupants(advance(seat_of, slots), slots)
    rot = exchange(gram_call(gradient, first, pairs), pairs)
    moved, band = middle_call(gradient, first, rot, pairs)
    rot = exchange(band, pairs)
    return last_call(moved, second, rot, pairs)


def solution(mesh):
    in_specs = (P(("wide", "narrow"), None), P())
    out_specs = P(("wide", "narrow"), None)
    return jax.shard_map(
        per_device, mesh=mesh, in_specs=in_specs, out_specs=out_specs, check_vma=False
    )
```

time: 1020 us -> 711 us (0.70)
  local copies, waits for them, and re-layouts: 232 us -> 2.75 us
  blocking collectives: 251 us -> 76.1 us
  waiting for transfers between devices: 406 us -> 510 us
  Pallas kernels: 0 us -> 102 us
  other arithmetic: 65.9 us -> 2.03 us
  starting transfers between devices: 25.9 us -> 0.04 us
  matrix products: 22.9 us -> 0 us
    psum x2, waiting for transfers between devices: 169 us -> 510 us  [exchange(): total = lax.psum(band, ('wide', 'narrow'))]
    all_to_all x2 -> x0, blocking collectives: 251 us -> none  [the longest x1 129 us: per_device(): lax.all_to_all(seated, 'wide', split_axis=1, concat_axis=0, tiled=True)]
    all_to_all x2 -> x0, waiting for transfers between devices: 237 us -> none  [per_device(): lax.all_to_all(paired.reshape(count_wide * row_count, 1, 2, block_width),...]
    gather x52 -> x0, local copies, waits for them, and re-layouts: 130 us -> none  [the longest x16 37.5 us: one_round(): off_diag = jnp.diagonal(gram_mat[:width, width:])]
    pallas_call x0 -> x5, Pallas kernels: none -> 102 us  [the longest x1 43.2 us: last_call(): pl.pallas_call(functools.partial(last_kernel, pairs), out_shape=jax.Shape...]
    all_gather x0 -> x2, blocking collectives: none -> 76.1 us  [exchange(): return lax.all_gather(rounds_call(mine), 'wide', axis=0, tiled=False)]
    reshape x6 -> x0, local copies, waits for them, and re-layouts: 56 us -> none  [the longest x2 27.2 us: per_device(): paired.reshape(count_wide * row_count, 1, 2, block_width)]
    all_to_all x2 -> x0, starting transfers between devices: 25.7 us -> none  [per_device(): lax.all_to_all(paired.reshape(count_wide * row_count, 1, 2, block_width),...]
  transfers between devices with their start and end apart: 4 -> 2, of which waited for: 4 -> 2; matrix products, arithmetic and copies ran while one was open for 0% -> 0% of each run, Pallas kernels for 0% -> 0%
where the time goes in v1:
time: 711 us; the launch traced here: 707 us
  waiting for transfers between devices  510 us (72%)
  Pallas kernels  102 us (14%)
  blocking collectives  76.1 us (11%)
  between operations  13.4 us (2%)
    psum x2, waiting for transfers between devices, exchange(): total = lax.psum(band, ('wide', 'narrow'))  510 us
    all_gather x2, blocking collectives, exchange(): return lax.all_gather(rounds_call(mine), 'wide', axis=0, tiled=False)  76.1 us
    pallas_call x1, Pallas kernels, last_call(): pl.pallas_call(functools.partial(last_kernel, pairs), out_shape=jax.Shape...  43.2 us
    pallas_call x1, Pallas kernels, middle_call(): pl.pallas_call(functools.partial(middle_kernel, pairs), out_shape=(jax.Sh...  29.2 us
    pallas_call x1, Pallas kernels, gram_call(): pl.pallas_call(gram_kernel, out_shape=jax.ShapeDtypeStruct((pairs, 32, BW...  22.3 us
  transfers between devices with their start and end apart: 2, of which 2 were waited for; matrix products, arithmetic and copies ran while one was open for 0% of the time, Pallas kernels for 0%

profile of v1, /device:TPU:1, one launch (start us, length us, event | category | flops | bytes accessed | tf_op | source)
XLA Modules:
  0.0 706.7 jit_solution(10652651329290412149)
XLA Ops:
  6.5 0.0 all-reduce.3.cloned.1.call-start
  6.5 1.4 select_reduce_fusion.hold
  7.9 22.3 %shard_map.28 = f32[32,32,256]{2,1,0:T(8,128)} custom-call(s32[64]{0:T(128)} %select_reduce_fusion.hold, bf16[160,16384]{1,0:T(8,128)(2,1)} %r_ref.3, bf16[160,16384]{1,0:T(8,128)(2,1)} %r_ref.3), custom_call_target="tpu_custom_call" | custom-call | tf_op jit(solution)/shard_map/pallas_call | solution.py:229
  30.2 0.0 all-reduce.3.cloned.1.call-update
  30.2 0.0 all-reduce.5.cloned.1.call-start
  30.3 258.2 %all-reduce.3.cloned.1.call-done = f32[32,32,256]{2,1,0:T(8,128)} async-done(((f32[32,32,256]{2,1,0:T(8,128)}), f32[32,32,256]{2,1,0:T(8,128)}) %all-reduce.3.cloned.1.call-update) | async-done | bytes 1048592 | tf_op jit(solution)/shard_map/psum | solution.py:302
  288.5 1.4 dynamic-slice_bitcast_fusion.1.in_ref
  289.8 3.7 shard_map.29
  293.6 38.1 %all-gather = bf16[1024,256]{1,0:T(8,128)(2,1)} all-gather(bf16[32,256]{1,0:T(8,128)(2,1)} %shard_map.29), channel_id=2, replica_groups=mesh['wide'=32,'narrow'=8] {'wide'}, dimensions={0}, use_global_device_ids=true | all-gather | bytes 540672 | tf_op jit(solution)/shard_map/all_gather | solution.py:304
  331.6 0.0 copy-start
  331.6 29.2 %shard_map.30 = (bf16[160,16384]{1,0:T(8,128)(2,1)}, f32[32,32,256]{2,1,0:T(8,128)}) custom-call(s32[64]{0:T(128)} %select_reduce_fusion.hold, bf16[160,16384]{1,0:T(8,128)(2,1)} %r_ref.3, bf16[160,16384]{1,0:T(8,128)(2,1)} %r_ref.3, bf16[32,32,256]{2,1,0:T(8,128)(2,1)} %bitcast.6), custom_call_target="tpu_custom_call" | custom-call | tf_op jit(solution)/shard_map/pallas_call | solution.py:248
  360.8 0.0 all-reduce.5.cloned.1.call-update
  360.9 0.0 copy-done
  360.9 0.6 select_reduce_fusion.1.hold
  361.5 251.9 %all-reduce.5.cloned.1.call-done = f32[32,32,256]{2,1,0:T(8,128)} async-done(((f32[32,32,256]{2,1,0:T(8,128)}), f32[32,32,256]{2,1,0:T(8,128)}) %all-reduce.5.cloned.1.call-update) | async-done | bytes 1048592 | tf_op jit(solution)/shard_map/psum | solution.py:302
  613.5 1.4 dynamic-slice_bitcast_fusion.in_ref
  614.8 3.7 shard_map.31
  618.6 38.1 %all-gather.1 = bf16[1024,256]{1,0:T(8,128)(2,1)} all-gather(bf16[32,256]{1,0:T(8,128)(2,1)} %shard_map.31), channel_id=3, replica_groups=mesh['wide'=32,'narrow'=8] {'wide'}, dimensions={0}, use_global_device_ids=true | all-gather | bytes 540672 | tf_op jit(solution)/shard_map/all_gather | solution.py:304
  656.6 43.2 %shard_map.32 = bf16[160,16384]{1,0:T(8,128)(2,1)} custom-call(s32[64]{0:T(128)} %select_reduce_fusion.1.hold, bf16[160,16384]{1,0:T(8,128)(2,1)} %get-tuple-element.7.l_ref.r_ref, bf16[160,16384]{1,0:T(8,128)(2,1)} %get-tuple-element.7.l_ref.r_ref, bf16[32,32,256]{2,1,0:T(8,128)(2,1)} %bitcast.7), custom_call_target="tpu_custom_call" | custom-call | tf_op jit(solution)/shard_map/pallas_call | solution.py:277
  (1 shorter events, 0.0 us)
Async XLA Ops:
  6.5 281.9 %all-reduce.3.cloned.1.call-start = ((), (), s32[]{:S(2)}) async-start(), calls=%async_computation | async-start | bytes 2097152 | tf_op jit(solution)/shard_map/psum | solution.py:302
  30.2 583.2 %all-reduce.5.cloned.1.call-start = ((), (), s32[]{:S(2)}) async-start(), calls=%async_computation.1 | async-start | bytes 2097152 | tf_op jit(solution)/shard_map/psum | solution.py:302
  331.6 29.3 %copy-start = (s32[64]{0:T(128)S(1)}, s32[64]{0:T(128)}, u32[]{:S(2)}) copy-start(s32[64]{0:T(128)} %param.3) | copy-start | bytes 772
Sparse Core Ops, SparseCore 0:
  30.4 258.0 all-reduce.2
  361.0 252.4 all-reduce.4

commit v2 on v1

v2 whole, which is shorter than its diff:
```python
import functools

import jax
import jax.numpy as jnp
from jax import lax
from jax.experimental import pallas as pl
from jax.experimental.pallas import tpu as pltpu
from jax.sharding import PartitionSpec as P

ROUNDS = 8
BW = 256
F32 = jnp.float32
BF16 = jnp.bfloat16


def advance(seat_of, total_slots):
    pair_count = total_slots // 2
    cycle_pos = jnp.where(seat_of % 2 == 0, seat_of // 2 - 1, total_slots - 2 - (seat_of - 1) // 2)
    next_pos = (cycle_pos + 1) % (total_slots - 1)
    new_slot = jnp.where(
        next_pos < pair_count - 1, 2 * (next_pos + 1), 2 * (total_slots - 2 - next_pos) + 1
    )
    return jnp.where(seat_of == 0, 0, new_slot)


def occupants(seat_of, total_slots):
    block_ids = jnp.arange(total_slots, dtype=jnp.int32)
    matches = seat_of[None, :] == block_ids[:, None]
    return jnp.sum(jnp.where(matches, block_ids[None, :], 0), axis=1).astype(jnp.int32)


def init_masks(mask_ref):
    s = lax.broadcasted_iota(jnp.int32, (8, 128), 0)
    c = lax.broadcasted_iota(jnp.int32, (8, 128), 1)
    for t in range(-1, 17):
        d = 8 * t + s - c
        mask_ref[t + 1] = jnp.where((d >= -7) & (d <= 7), 1.0, 0.0).astype(F32)
    for t in range(17):
        d = 8 * t + s - c
        mask_ref[18 + t] = jnp.where((d >= 0) & (d <= 7), 1.0, 0.0).astype(F32)


def dot_t(a, b):
    return lax.dot_general(a, b, (((0,), (0,)), ((), ())), preferred_element_type=F32)


def gram_band(left, right, mask_ref, g_ref, out_ref):
    g_ref[0] = dot_t(left, right)
    g_ref[1] = dot_t(left, left)
    g_ref[2] = dot_t(right, right)
    for j in range(2):
        lanes = slice(128 * j, 128 * j + 128)
        acc = [jnp.zeros((8, 128), F32) for _ in range(4)]
        for t in range(-1, 17):
            u = (16 * j + t) % 32
            acc[u % 2] += g_ref[0, 8 * u : 8 * u + 8, lanes] * mask_ref[t + 1]
        for t in range(17):
            u = (16 * j + t) % 32
            mask = mask_ref[18 + t]
            acc[2 + u % 2] += g_ref[1, 8 * u : 8 * u + 8, lanes] * mask
            acc[2 + (u + 1) % 2] += g_ref[2, 8 * u : 8 * u + 8, lanes] * mask
        for r in range(4):
            out_ref[8 * r : 8 * r + 8, lanes] = acc[r]


def lane_roll(x, back):
    return pltpu.roll(x, (-back) % x.shape[1], 1)


def row_roll(x, down):
    return pltpu.roll(x, down % x.shape[0], 0)


def iota(shape, axis):
    return lax.broadcasted_iota(jnp.int32, shape, axis)


def skew(x, sign):
    c = iota(x.shape, 1)
    for b in (1, 2, 4, 8):
        x = jnp.where((c & b) != 0, row_roll(x, sign * b), x)
    return x


def spread(x):
    y = jnp.broadcast_to(x, (8, x.shape[1]))
    d = iota(y.shape, 0)
    for b in (1, 2, 4):
        y = jnp.where((d & b) != 0, lane_roll(y, b), y)
    return y


def rotation_band(band):
    cross = skew(band[:16], -1)
    own = skew(band[16:], -1)
    lr = cross[:8]
    ll = own[:8]
    rr = own[8:]
    d = iota((8, BW), 0)
    flipped = [lr[0:1]] + [lane_roll(cross[16 - k : 17 - k], k) for k in range(1, 8)]
    rl = jnp.concatenate(flipped, axis=0)
    ca = jnp.where(d == 0, 1.0, 0.0).astype(F32)
    cb = jnp.zeros((8, BW), F32)
    cc = jnp.zeros((8, BW), F32)
    cd = ca
    for r in range(ROUNDS):
        a = ll[0:1]
        c = rr[0:1]
        off = lr[0:1]
        spread_ac = c - a
        damp = (a + c) / 16.0 + 1e-06
        radius = jnp.sqrt(spread_ac * spread_ac + 4.0 * off * off + damp * damp)
        tangent = 2.0 * off / (spread_ac + radius)
        cs = 1.0 / jnp.sqrt(1.0 + tangent * tangent)
        sn = tangent * cs
        if r < ROUNDS - 1:
            csd = spread(cs)
            snd = spread(sn)
            ll1 = ll * cs - lr * sn
            lr1 = ll * sn + lr * cs
            rl1 = rl * cs - rr * sn
            rr1 = rl * sn + rr * cs
            ll = csd * ll1 - snd * rl1
            rl = snd * ll1 + csd * rl1
            lr = csd * lr1 - snd * rr1
            rr = snd * lr1 + csd * rr1
        ca, cc = cs * ca - sn * cc, sn * ca + cs * cc
        cb, cd = cs * cb - sn * cd, sn * cb + cs * cd
        if r < ROUNDS - 1:
            lr = jnp.where(d == 0, row_roll(rl, -1), row_roll(lane_roll(lr, 1), 1))
            rl = jnp.where(d == 7, 0.0, row_roll(rl, -1))
            rr = lane_roll(rr, 1)
            cc = jnp.where(d == 0, 0.0, row_roll(lane_roll(cc, 1), 1))
            cd = jnp.where(d == 0, 0.0, row_roll(lane_roll(cd, 1), 1))
    first = jnp.concatenate([ca, cb], axis=0)
    second = row_roll(jnp.concatenate([lane_roll(cd, -7), lane_roll(cc, -7)], axis=0), 1)
    return jnp.concatenate([skew(first, 1), skew(second, 1)], axis=0)


def build_dense(rot, m_ref):
    wide = rot.astype(F32)
    s = iota((16, 128), 0)
    c = iota((16, 128), 1)
    for half in range(2):
        part = wide[16 * half : 16 * half + 16]
        turned = jnp.concatenate([part[8:], part[:8]], axis=0)
        for j in range(2):
            lanes = slice(128 * j, 128 * j + 128)
            out_lanes = slice(256 * half + 128 * j, 256 * half + 128 * j + 128)
            for g in (range(0, 9) if half == 0 else range(-1, 8)):
                d = 16 * g + s - c
                keep = ((d >= 0) & (d <= 7)) if half == 0 else ((d >= -7) & (d <= 0))
                row = 16 * ((g + 8 * j) % 16)
                m_ref[row : row + 16, out_lanes] = jnp.where(keep, part[:, lanes], 0.0).astype(BF16)
                m_ref[256 + row : 256 + row + 16, out_lanes] = jnp.where(
                    keep, turned[:, lanes], 0.0
                ).astype(BF16)


def apply_dense(left, right, m_ref):
    new = jnp.dot(left, m_ref[:256], preferred_element_type=F32)
    return (new + jnp.dot(right, m_ref[256:], preferred_element_type=F32)).astype(BF16)


MESH = pl.DeviceIdType.MESH
CHUNKS = 8
TOP, LOW = slice(0, 16), slice(16, 32)


def place():
    w = lax.axis_index("wide")
    n = lax.axis_index("narrow")
    z, y_lo, core = w // 4, (w // 2) % 2, w % 2
    x, y_hi = n // 2, n % 2
    return x, 2 * y_hi + y_lo, z, core


def device(x, y, z, core):
    return ((z * 2 + y % 2) * 2 + core, x * 2 + y // 2)


def seats_before(q, pairs):
    return jnp.maximum(2 * q - 2, q), 2 * q + 3 - 3 * (q // (pairs - 1))


def block(seat):
    return pl.ds(pl.multiple_of(seat * BW, BW), BW)


def main_kernel(
    pairs,
    hold,
    x_hbm,
    y_hbm,
    rot_out,
    x_ref,
    y_ref,
    mask_ref,
    g_ref,
    m_ref,
    rot_in,
    band,
    r1,
    acc1,
    ra2,
    rb2,
    acca,
    accb,
    ra3,
    rb3,
    mine,
    rz,
    load_sem,
    store_sem,
    send_sem,
    recv_sem,
):
    half = pairs // 2
    x, y, z, core = place()
    partner = device(x, y, z, 1 - core)
    along_x = [device((x + k) % 4, y, z, core) for k in range(1, 4)]
    along_y = [device(x, (y + k) % 4, z, core) for k in range(1, 4)]
    along_z = [device(x, y, (z + k) % 8, core) for k in range(1, 8)]
    width = y_ref.shape[1] // CHUNKS

    def start(copies):
        for copy in copies:
            copy.start()

    def finish(copies):
        for copy in copies:
            copy.wait()

    loads = []
    stores = []
    for k in range(CHUNKS):
        cols = slice(k * width, (k + 1) * width)
        stores.append(pltpu.make_async_copy(y_ref.at[:, cols], y_hbm.at[:, cols], store_sem.at[k]))
    for k in range(2 * pairs):
        cols = slice(k * BW, (k + 1) * BW)
        loads.append(pltpu.make_async_copy(x_hbm.at[:, cols], x_ref.at[k], load_sem.at[k]))
    start(loads)

    barrier = pltpu.get_barrier_semaphore()
    greeted = [partner] + along_x + along_y + along_z
    for other in greeted:
        pl.semaphore_signal(barrier, inc=1, device_id=other, device_id_type=MESH)

    init_masks(mask_ref)
    m_ref[...] = jnp.zeros_like(m_ref)
    finish(loads)
    pl.semaphore_wait(barrier, len(greeted))

    for step in range(2):

        def remote(index, src, dst, target):
            return pltpu.make_async_remote_copy(
                src_ref=src,
                dst_ref=dst,
                send_sem=send_sem.at[step, index],
                recv_sem=recv_sem.at[step, index],
                device_id=target,
                device_id_type=MESH,
            )

        rot = rot_in if step == 0 else rot_out

        def gram_half(side):
            def body(i, carry):
                for k in range(2):
                    j = 2 * i + k
                    p = side * half + j
                    if step == 0:
                        left = x_ref[hold[2 * p]]
                        right = x_ref[hold[2 * p + 1]]
                    else:
                        a, b = seats_before(p, pairs)
                        left = y_ref[:, block(a)]
                        right = y_ref[:, block(b)]
                    gram_band(
                        left, right, mask_ref, g_ref.at[k], band.at[step, side, j // 4, j % 4]
                    )
                return carry

            lax.fori_loop(0, half // 2, body, 0)

        gram_half(1 - core)
        swap = [remote(0, band.at[step, 1 - core], r1.at[step], partner)]
        start(swap)
        gram_half(core)
        finish(swap)
        acc1[...] = band[step, core] + r1[step]

        copies = []
        for k in range(1, 4):
            copies.append(
                remote(k, acc1.at[(x + k) % 4, :, TOP], ra2.at[step, k - 1], along_x[k - 1])
            )
            copies.append(
                remote(3 + k, acc1.at[:, (y + k) % 4, LOW], rb2.at[step, k - 1], along_y[k - 1])
            )
        start(copies)
        finish(copies)
        acca[...] = (acc1[x, :, TOP] + ra2[step, 0]) + (ra2[step, 1] + ra2[step, 2])
        accb[...] = (acc1[:, y, LOW] + rb2[step, 0]) + (rb2[step, 1] + rb2[step, 2])

        copies = []
        for k in range(1, 4):
            copies.append(
                remote(6 + k, acca.at[(y + k) % 4], ra3.at[step, k - 1], along_y[k - 1])
            )
            copies.append(
                remote(9 + k, accb.at[(x + k) % 4], rb3.at[step, k - 1], along_x[k - 1])
            )
        start(copies)
        finish(copies)
        mine[TOP] = (acca[y] + ra3[step, 0]) + (ra3[step, 1] + ra3[step, 2])
        mine[LOW] = (accb[x] + rb3[step, 0]) + (rb3[step, 1] + rb3[step, 2])

        copies = [remote(12 + k, mine, rz.at[step, z], along_z[k - 1]) for k in range(1, 8)]
        start(copies)
        rz[step, z] = mine[...]
        finish(copies)
        total = ((rz[step, 0] + rz[step, 1]) + (rz[step, 2] + rz[step, 3])) + (
            (rz[step, 4] + rz[step, 5]) + (rz[step, 6] + rz[step, 7])
        )

        rot[core, x, y] = rotation_band(total).astype(BF16)

        copies = []
        for k in range(1, 4):
            piece = rot.at[core, x, y, TOP]
            copies.append(remote(19 + k, piece, piece, along_y[k - 1]))
            piece = rot.at[core, x, y, LOW]
            copies.append(remote(22 + k, piece, piece, along_x[k - 1]))
        start(copies)
        finish(copies)
        copies = []
        for k in range(1, 4):
            piece = rot.at[core, x, :, TOP]
            copies.append(remote(25 + k, piece, piece, along_x[k - 1]))
            piece = rot.at[core, :, y, LOW]
            copies.append(remote(28 + k, piece, piece, along_y[k - 1]))
        start(copies)
        finish(copies)
        swap = [remote(32, rot.at[core], rot.at[core], partner)]
        start(swap)
        if step == 1:
            finish(swap)
            finish(stores)
            break

        def apply_half(side):
            def body(i, carry):
                for k in range(2):
                    j = 2 * i + k
                    p = side * half + j
                    build_dense(rot[side, j // 4, j % 4], m_ref.at[k])
                    left = x_ref[hold[2 * p]]
                    right = x_ref[hold[2 * p + 1]]
                    cols = pl.ds(pl.multiple_of(p * 2 * BW, 2 * BW), 2 * BW)
                    y_ref[:, cols] = apply_dense(left, right, m_ref.at[k])
                return carry

            lax.fori_loop(0, half // 2, body, 0)

        apply_half(core)
        finish(swap)
        apply_half(1 - core)
        start(stores)


def main_call(x, holders, pairs):
    rows, cols = x.shape
    vmem = pl.BlockSpec(memory_space=pltpu.VMEM)
    hbm = pl.BlockSpec(memory_space=pl.ANY)
    out, rot = pl.pallas_call(
        functools.partial(main_kernel, pairs),
        out_shape=(
            jax.ShapeDtypeStruct((rows, cols), BF16),
            jax.ShapeDtypeStruct((2, 4, 4, 32, BW), BF16),
        ),
        in_specs=[pl.BlockSpec(memory_space=pltpu.SMEM), hbm],
        out_specs=(hbm, vmem),
        scratch_shapes=[
            pltpu.VMEM((2 * pairs, rows, BW), BF16),
            pltpu.VMEM((rows, cols), BF16),
            pltpu.VMEM((35, 8, 128), F32),
            pltpu.VMEM((2, 3, BW, BW), F32),
            pltpu.VMEM((2, 2 * BW, 2 * BW), BF16),
            pltpu.VMEM((2, 4, 4, 32, BW), BF16),
            pltpu.VMEM((2, 2, 4, 4, 32, BW), F32),
            pltpu.VMEM((2, 4, 4, 32, BW), F32),
            pltpu.VMEM((4, 4, 32, BW), F32),
            pltpu.VMEM((2, 3, 4, 16, BW), F32),
            pltpu.VMEM((2, 3, 4, 16, BW), F32),
            pltpu.VMEM((4, 16, BW), F32),
            pltpu.VMEM((4, 16, BW), F32),
            pltpu.VMEM((2, 3, 16, BW), F32),
            pltpu.VMEM((2, 3, 16, BW), F32),
            pltpu.VMEM((32, BW), F32),
            pltpu.VMEM((2, 8, 32, BW), F32),
            pltpu.SemaphoreType.DMA((2 * pairs,)),
            pltpu.SemaphoreType.DMA((CHUNKS,)),
            pltpu.SemaphoreType.DMA((2, 33)),
            pltpu.SemaphoreType.DMA((2, 33)),
        ],
        compiler_params=pltpu.CompilerParams(collective_id=0, has_side_effects=True),
    )(holders, x)
    return out, rot.reshape(pairs, 32, BW)


def last_kernel(pairs, hold, y_hbm, rot, out_hbm, y_ref, m_ref, z_ref, load_sem, store_sem):
    width = y_ref.shape[1] // CHUNKS
    per_chunk = pairs // CHUNKS

    def load(k):
        cols = pl.ds(pl.multiple_of(k * width, width), width)
        return pltpu.make_async_copy(y_hbm.at[:, cols], y_ref.at[:, cols], load_sem.at[k])

    def store(seat):
        return pltpu.make_async_copy(
            z_ref.at[:, block(seat)], out_hbm.at[:, block(hold[seat])], store_sem.at[seat]
        )

    for k in range(CHUNKS):
        load(k).start()
    m_ref[...] = jnp.zeros_like(m_ref)
    load(0).wait()

    def body(i, carry):
        @pl.when(i + 1 < CHUNKS)
        def _():
            load(i + 1).wait()

        def inner(h, carry):
            for k in range(2):
                q = i * per_chunk + 2 * h + k
                build_dense(rot[q], m_ref.at[k])
                a, b = seats_before(q, pairs)
                cols = pl.ds(pl.multiple_of(q * 2 * BW, 2 * BW), 2 * BW)
                z_ref[:, cols] = apply_dense(y_ref[:, block(a)], y_ref[:, block(b)], m_ref.at[k])
                store(2 * q).start()
                store(2 * q + 1).start()
            return carry

        return lax.fori_loop(0, per_chunk // 2, inner, carry)

    lax.fori_loop(0, CHUNKS, body, 0)

    def drain(seat, carry):
        store(seat).wait()
        return carry

    lax.fori_loop(0, 2 * pairs, drain, 0)


def last_call(y, holders, rot, pairs):
    rows, cols = y.shape
    vmem = pl.BlockSpec(memory_space=pltpu.VMEM)
    hbm = pl.BlockSpec(memory_space=pl.ANY)
    return pl.pallas_call(
        functools.partial(last_kernel, pairs),
        out_shape=jax.ShapeDtypeStruct((rows, cols), BF16),
        in_specs=[pl.BlockSpec(memory_space=pltpu.SMEM), hbm, vmem],
        out_specs=hbm,
        scratch_shapes=[
            pltpu.VMEM((rows, cols), BF16),
            pltpu.VMEM((2, 2 * BW, 2 * BW), BF16),
            pltpu.VMEM((rows, cols), BF16),
            pltpu.SemaphoreType.DMA((CHUNKS,)),
            pltpu.SemaphoreType.DMA((2 * pairs,)),
        ],
    )(holders, y, rot)


def per_device(gradient, seating):
    slots = gradient.shape[1] // BW
    pairs = slots // 2
    seat_of = seating.astype(jnp.int32)
    first = occupants(seat_of, slots)
    second = occupants(advance(seat_of, slots), slots)
    moved, rot = main_call(gradient, first, pairs)
    return last_call(moved, second, rot, pairs)


def solution(mesh):
    in_specs = (P(("wide", "narrow"), None), P())
    out_specs = P(("wide", "narrow"), None)
    return jax.shard_map(
        per_device, mesh=mesh, in_specs=in_specs, out_specs=out_specs, check_vma=False
    )
```

time: 711 us -> 98.9 us (0.14)
  waiting for transfers between devices: 510 us -> 0 us
  blocking collectives: 76.1 us -> 0 us
  between operations: 13.4 us -> 0.01 us
    psum x2 -> x0, waiting for transfers between devices: 510 us -> none  [exchange(): total = lax.psum(band, ('wide', 'narrow'))]
    all_gather x2 -> x0, blocking collectives: 76.1 us -> none  [exchange(): return lax.all_gather(rounds_call(mine), 'wide', axis=0, tiled=False)]
    pallas_call x1, Pallas kernels: 43.2 us -> 10.1 us  [last_call(): pl.pallas_call(functools.partial(last_kernel, pairs), out_shape=jax.Shape...]
    pallas_call x4 -> x1, Pallas kernels: 59 us -> 86 us  [main_call(): pl.pallas_call(functools.partial(main_kernel, pairs), out_shape=(jax.Shap...]
  transfers between devices with their start and end apart: 2 -> 0, of which waited for: 2 -> 0; matrix products, arithmetic and copies ran while one was open for 0% -> 0% of each run, Pallas kernels for 0% -> 0%
where the time goes in v2:
time: 98.9 us; the launch traced here: 98.7 us
  Pallas kernels  96 us (97%)
  other arithmetic  2.67 us (3%)
    pallas_call x1, Pallas kernels, main_call(): pl.pallas_call(functools.partial(main_kernel, pairs), out_shape=(jax.Shap...  86 us
    pallas_call x1, Pallas kernels, last_call(): pl.pallas_call(functools.partial(last_kernel, pairs), out_shape=jax.Shape...  10.1 us
    reduce_sum x2, other arithmetic, occupants(): jnp.sum(jnp.where(matches, block_ids[None, :], 0), axis=1).astype(jnp.int32)  1.99 us

profile of v2, /device:TPU:1, one launch (start us, length us, event | category | flops | bytes accessed | tf_op | source)
XLA Modules:
  0.0 98.7 jit_solution(17782580736453315113)
XLA Ops:
  0.0 1.3 %select_reduce_fusion.hold = s32[64]{0:T(128)} fusion(s32[64]{0:T(128)} %param.3), kind=kLoop, calls=%fused_computation | loop fusion | flops 12224 | bytes 512 | tf_op jit(solution)/shard_map/reduce_sum | solution.py:29
  1.3 0.7 compare_select_fusion.2
  2.0 0.7 select_reduce_fusion.1.hold
  2.7 86.0 %shard_map.28 = (bf16[160,16384]{1,0:T(8,128)(2,1)}, bf16[2,4,4,32,256]{4,3,2,1,0:T(8,128)(2,1)}) custom-call(s32[64]{0:T(128)} %select_reduce_fusion.hold, bf16[160,16384]{1,0:T(8,128)(2,1)} %x_hbm.1), custom_call_target="tpu_custom_call" | custom-call | tf_op jit(solution)/shard_map/pallas_call | solution.py:377
  88.7 10.1 %shard_map.29 = bf16[160,16384]{1,0:T(8,128)(2,1)} custom-call(s32[64]{0:T(128)} %select_reduce_fusion.1.hold, bf16[160,16384]{1,0:T(8,128)(2,1)} %get-tuple-element.7.y_hbm, bf16[32,32,256]{2,1,0:T(8,128)(2,1)} %bitcast.1), custom_call_target="tpu_custom_call" | custom-call | tf_op jit(solution)/shard_map/pallas_call | solution.py:462

commit v3 on v2

--- a/solution.py
+++ b/solution.py
@@ -164,6 +164,7 @@
 
 MESH = pl.DeviceIdType.MESH
 CHUNKS = 8
+SWAP, FIRST_X, FIRST_Y, SECOND, ALONG_Z, PLANE, FORWARD, COPIES = 0, 4, 16, 32, 38, 46, 62, 78
 TOP, LOW = slice(0, 16), slice(16, 32)
 
 
@@ -242,14 +243,14 @@
     start(loads)
 
     barrier = pltpu.get_barrier_semaphore()
-    greeted = [partner] + along_x + along_y + along_z
+    plane = [device((x + i // 4) % 4, (y + i % 4) % 4, z, core) for i in range(1, 16)]
+    greeted = [partner] + plane + along_z
     for other in greeted:
         pl.semaphore_signal(barrier, inc=1, device_id=other, device_id_type=MESH)
 
     init_masks(mask_ref)
     m_ref[...] = jnp.zeros_like(m_ref)
     finish(loads)
-    pl.semaphore_wait(barrier, len(greeted))
 
     for step in range(2):
 
@@ -265,59 +266,107 @@
 
         rot = rot_in if step == 0 else rot_out
 
-        def gram_half(side):
-            def body(i, carry):
+        def gram_pairs(side, pieces):
+            for k, (i, j) in enumerate(pieces):
+                p = side * half + 4 * i + j
+                if step == 0:
+                    left = x_ref[hold[2 * p]]
+                    right = x_ref[hold[2 * p + 1]]
+                else:
+                    a, b = seats_before(p, pairs)
+                    left = y_ref[:, block(a)]
+                    right = y_ref[:, block(b)]
+                gram_band(left, right, mask_ref, g_ref.at[k], band.at[step, side, i, j])
+
+        def ahead(base, i):
+            return lax.rem(base + i + 1, 4)
+
+        def swap(g):
+            group = ahead(x, g)
+            return remote(SWAP + g, band.at[step, 1 - core, group], r1.at[step, group], partner)
+
+        def theirs(g, carry):
+            def body(h, carry):
+                gram_pairs(1 - core, [(ahead(x, g), 2 * h), (ahead(x, g), 2 * h + 1)])
+                return carry
+
+            lax.fori_loop(0, 2, body, 0)
+            if step == 0:
+
+                @pl.when(g == 0)
+                def _():
+                    pl.semaphore_wait(barrier, len(greeted))
+
+            swap(g).start()
+            return carry
+
+        lax.fori_loop(0, 4, theirs, 0)
+
+        def top(g, h):
+            i, j = ahead(x, g), ahead(y, h)
+            return remote(
+                FIRST_X + 4 * g + h, acc1.at[i, j, TOP], ra2.at[step, g, j], device(i, y, z, core)
+            )
+
+        def low(g, h):
+            i, j = ahead(x, g), ahead(y, h)
+            return remote(
+                FIRST_Y + 4 * g + h, acc1.at[i, j, LOW], rb2.at[step, h, i], device(x, j, z, core)
+            )
+
+        def ours(g, carry):
+            i = ahead(x, g)
+
+            def body(h2, carry):
+                gram_pairs(core, [(i, ahead(y, 2 * h2)), (i, ahead(y, 2 * h2 + 1))])
+
+                @pl.when(h2 == 0)
+                def _():
+                    swap(g).wait()
+
                 for k in range(2):
-                    j = 2 * i + k
-                    p = side * half + j
-                    if step == 0:
-                        left = x_ref[hold[2 * p]]
-                        right = x_ref[hold[2 * p + 1]]
-                    else:
-                        a, b = seats_before(p, pairs)
-                        left = y_ref[:, block(a)]
-                        right = y_ref[:, block(b)]
-                    gram_band(
-                        left, right, mask_ref, g_ref.at[k], band.at[step, side, j // 4, j % 4]
-                    )
+                    h = 2 * h2 + k
+                    j = ahead(y, h)
+                    acc1[i, j] = band[step, core, i, j] + r1[step, i, j]
+
+                    @pl.when(g < 3)
+                    def _():
+                        top(g, h).start()
+
+                    @pl.when(h < 3)
+                    def _():
+                        low(g, h).start()
+
                 return carry
 
-            lax.fori_loop(0, half // 2, body, 0)
-
-        gram_half(1 - core)
-        swap = [remote(0, band.at[step, 1 - core], r1.at[step], partner)]
-        start(swap)
-        gram_half(core)
-        finish(swap)
-        acc1[...] = band[step, core] + r1[step]
+            return lax.fori_loop(0, 2, body, carry)
+
+        lax.fori_loop(0, 4, ours, 0)
+
+        def arrived(n, carry):
+            a, b = n // 4, lax.rem(n, 4)
+            top(a, b).wait()
+            low(b, a).wait()
+            return carry
+
+        lax.fori_loop(0, 12, arrived, 0)
+        acca[...] = (acc1[x, :, TOP] + ra2[step, 0]) + (ra2[step, 1] + ra2[step, 2])
+        accb[...] = (acc1[:, y, LOW] + rb2[step, 0]) + (rb2[step, 1] + rb2[step, 2])
 
         copies = []
         for k in range(1, 4):
             copies.append(
-                remote(k, acc1.at[(x + k) % 4, :, TOP], ra2.at[step, k - 1], along_x[k - 1])
+                remote(SECOND + k, acca.at[(y + k) % 4], ra3.at[step, k - 1], along_y[k - 1])
             )
             copies.append(
-                remote(3 + k, acc1.at[:, (y + k) % 4, LOW], rb2.at[step, k - 1], along_y[k - 1])
-            )
-        start(copies)
-        finish(copies)
-        acca[...] = (acc1[x, :, TOP] + ra2[step, 0]) + (ra2[step, 1] + ra2[step, 2])
-        accb[...] = (acc1[:, y, LOW] + rb2[step, 0]) + (rb2[step, 1] + rb2[step, 2])
-
-        copies = []
-        for k in range(1, 4):
-            copies.append(
-                remote(6 + k, acca.at[(y + k) % 4], ra3.at[step, k - 1], along_y[k - 1])
-            )
-            copies.append(
-                remote(9 + k, accb.at[(x + k) % 4], rb3.at[step, k - 1], along_x[k - 1])
+                remote(SECOND + 3 + k, accb.at[(x + k) % 4], rb3.at[step, k - 1], along_x[k - 1])
             )
         start(copies)
         finish(copies)
         mine[TOP] = (acca[y] + ra3[step, 0]) + (ra3[step, 1] + ra3[step, 2])
         mine[LOW] = (accb[x] + rb3[step, 0]) + (rb3[step, 1] + rb3[step, 2])
 
-        copies = [remote(12 + k, mine, rz.at[step, z], along_z[k - 1]) for k in range(1, 8)]
+        copies = [remote(ALONG_Z + k, mine, rz.at[step, z], along_z[k - 1]) for k in range(1, 8)]
         start(copies)
         rz[step, z] = mine[...]
         finish(copies)
@@ -327,47 +376,72 @@
 
         rot[core, x, y] = rotation_band(total).astype(BF16)
 
-        copies = []
-        for k in range(1, 4):
-            piece = rot.at[core, x, y, TOP]
-            copies.append(remote(19 + k, piece, piece, along_y[k - 1]))
-            piece = rot.at[core, x, y, LOW]
-            copies.append(remote(22 + k, piece, piece, along_x[k - 1]))
-        start(copies)
-        finish(copies)
-        copies = []
-        for k in range(1, 4):
-            piece = rot.at[core, x, :, TOP]
-            copies.append(remote(25 + k, piece, piece, along_x[k - 1]))
-            piece = rot.at[core, :, y, LOW]
-            copies.append(remote(28 + k, piece, piece, along_y[k - 1]))
-        start(copies)
-        finish(copies)
-        swap = [remote(32, rot.at[core], rot.at[core], partner)]
-        start(swap)
-        if step == 1:
-            finish(swap)
-            finish(stores)
-            break
-
-        def apply_half(side):
-            def body(i, carry):
+        def spread_out(i):
+            piece = rot.at[core, x, y]
+            return remote(PLANE + i, piece, piece, device((x + i // 4) % 4, (y + i % 4) % 4, z, core))
+
+        def source(i):
+            return lax.rem(x + 4 - i // 4, 4), lax.rem(y + 4 - lax.rem(i, 4), 4)
+
+        def arriving(i):
+            sx, sy = source(i)
+            piece = rot.at[core, sx, sy]
+            return remote(PLANE + i, piece, piece, partner)
+
+        def forward(i):
+            sx, sy = source(i)
+            piece = rot.at[core, sx, sy]
+            return remote(FORWARD + i, piece, piece, partner)
+
+        def forwarded(i):
+            sx, sy = source(i)
+            piece = rot.at[1 - core, sx, sy]
+            return remote(FORWARD + i, piece, piece, partner)
+
+        for i in range(1, 16):
+            spread_out(i).start()
+        forward(0).start()
+
+        def apply_pair(side, i, k):
+            sx, sy = source(i)
+            p = side * half + 4 * sx + sy
+            build_dense(rot[side, sx, sy], m_ref.at[k])
+            left = x_ref[hold[2 * p]]
+            right = x_ref[hold[2 * p + 1]]
+            cols = pl.ds(pl.multiple_of(p * 2 * BW, 2 * BW), 2 * BW)
+            y_ref[:, cols] = apply_dense(left, right, m_ref.at[k])
+
+        def first_half(h, carry):
+            for k in range(2):
+                i = 2 * h + k
+
+                @pl.when(i > 0)
+                def _():
+                    arriving(i).wait_recv()
+                    forward(i).start()
+
+            if step == 0:
                 for k in range(2):
-                    j = 2 * i + k
-                    p = side * half + j
-                    build_dense(rot[side, j // 4, j % 4], m_ref.at[k])
-                    left = x_ref[hold[2 * p]]
-                    right = x_ref[hold[2 * p + 1]]
-                    cols = pl.ds(pl.multiple_of(p * 2 * BW, 2 * BW), 2 * BW)
-                    y_ref[:, cols] = apply_dense(left, right, m_ref.at[k])
-                return carry
-
-            lax.fori_loop(0, half // 2, body, 0)
-
-        apply_half(core)
-        finish(swap)
-        apply_half(1 - core)
-        start(stores)
+                    apply_pair(core, 2 * h + k, k)
+            return carry
+
+        def second_half(h, carry):
+            for k in range(2):
+                forwarded(2 * h + k).wait_recv()
+            if step == 0:
+                for k in range(2):
+                    apply_pair(1 - core, 2 * h + k, k)
+            return carry
+
+        lax.fori_loop(0, 8, first_half, 0)
+        lax.fori_loop(0, 8, second_half, 0)
+        for i in range(1, 16):
+            spread_out(i).wait_send()
+        for i in range(16):
+            forward(i).wait_send()
+        if step == 0:
+            start(stores)
+    finish(stores)
 
 
 def main_call(x, holders, pairs):
@@ -402,8 +476,8 @@
             pltpu.VMEM((2, 8, 32, BW), F32),
             pltpu.SemaphoreType.DMA((2 * pairs,)),
             pltpu.SemaphoreType.DMA((CHUNKS,)),
-            pltpu.SemaphoreType.DMA((2, 33)),
-            pltpu.SemaphoreType.DMA((2, 33)),
+            pltpu.SemaphoreType.DMA((2, COPIES)),
+            pltpu.SemaphoreType.DMA((2, COPIES)),
         ],
         compiler_params=pltpu.CompilerParams(collective_id=0, has_side_effects=True),
     )(holders, x)

time: 98.9 us -> 92.3 us (0.933)
  Pallas kernels: 96 us -> 89.4 us
    pallas_call x1, Pallas kernels: 86 us -> 79.4 us  [main_call(): pl.pallas_call(functools.partial(main_kernel, pairs), out_shape=(jax.Shap...]
where the time goes in v3:
time: 92.3 us; the launch traced here: 92.1 us
  Pallas kernels  89.4 us (97%)
  other arithmetic  2.67 us (3%)
    pallas_call x1, Pallas kernels, main_call(): pl.pallas_call(functools.partial(main_kernel, pairs), out_shape=(jax.Shap...  79.4 us
    pallas_call x1, Pallas kernels, last_call(): pl.pallas_call(functools.partial(last_kernel, pairs), out_shape=jax.Shape...  10.1 us
    reduce_sum x2, other arithmetic, occupants(): jnp.sum(jnp.where(matches, block_ids[None, :], 0), axis=1).astype(jnp.int32)  1.99 us

profile of v3, /device:TPU:1, one launch (start us, length us, event | category | flops | bytes accessed | tf_op | source)
XLA Modules:
  0.0 92.1 jit_solution(14795591642074009359)
XLA Ops:
  0.0 1.3 %select_reduce_fusion.hold = s32[64]{0:T(128)} fusion(s32[64]{0:T(128)} %param.3), kind=kLoop, calls=%fused_computation | loop fusion | flops 12224 | bytes 512 | tf_op jit(solution)/shard_map/reduce_sum | solution.py:29
  1.3 0.7 compare_select_fusion.2
  2.0 0.7 select_reduce_fusion.1.hold
  2.7 79.4 %shard_map.28 = (bf16[160,16384]{1,0:T(8,128)(2,1)}, bf16[2,4,4,32,256]{4,3,2,1,0:T(8,128)(2,1)}) custom-call(s32[64]{0:T(128)} %select_reduce_fusion.hold, bf16[160,16384]{1,0:T(8,128)(2,1)} %x_hbm.1), custom_call_target="tpu_custom_call" | custom-call | tf_op jit(solution)/shard_map/pallas_call | solution.py:451
  82.1 10.1 %shard_map.29 = bf16[160,16384]{1,0:T(8,128)(2,1)} custom-call(s32[64]{0:T(128)} %select_reduce_fusion.1.hold, bf16[160,16384]{1,0:T(8,128)(2,1)} %get-tuple-element.7.y_hbm, bf16[32,32,256]{2,1,0:T(8,128)(2,1)} %bitcast.1), custom_call_target="tpu_custom_call" | custom-call | tf_op jit(solution)/shard_map/pallas_call | solution.py:536

commit v4 on v3

--- a/solution.py
+++ b/solution.py
@@ -137,24 +137,29 @@
     return jnp.concatenate([skew(first, 1), skew(second, 1)], axis=0)
 
 
-def build_dense(rot, m_ref):
-    wide = rot.astype(F32)
-    s = iota((16, 128), 0)
-    c = iota((16, 128), 1)
+def init_keep(keep_ref):
+    s = lax.broadcasted_iota(jnp.int32, (16, 128), 0)
+    c = lax.broadcasted_iota(jnp.int32, (16, 128), 1)
+    for t in range(9):
+        d = 16 * t + s - c
+        keep_ref[t] = jnp.where((d >= 0) & (d <= 7), 1.0, 0.0).astype(BF16)
+        d = 16 * (t - 1) + s - c
+        keep_ref[9 + t] = jnp.where((d >= -7) & (d <= 0), 1.0, 0.0).astype(BF16)
+
+
+def build_dense(rot, keep_ref, m_ref):
     for half in range(2):
-        part = wide[16 * half : 16 * half + 16]
-        turned = jnp.concatenate([part[8:], part[:8]], axis=0)
+        part = rot[16 * half : 16 * half + 16]
+        turned = part.astype(F32)
+        turned = jnp.concatenate([turned[8:], turned[:8]], axis=0).astype(BF16)
         for j in range(2):
             lanes = slice(128 * j, 128 * j + 128)
             out_lanes = slice(256 * half + 128 * j, 256 * half + 128 * j + 128)
-            for g in (range(0, 9) if half == 0 else range(-1, 8)):
-                d = 16 * g + s - c
-                keep = ((d >= 0) & (d <= 7)) if half == 0 else ((d >= -7) & (d <= 0))
-                row = 16 * ((g + 8 * j) % 16)
-                m_ref[row : row + 16, out_lanes] = jnp.where(keep, part[:, lanes], 0.0).astype(BF16)
-                m_ref[256 + row : 256 + row + 16, out_lanes] = jnp.where(
-                    keep, turned[:, lanes], 0.0
-                ).astype(BF16)
+            for t in range(9):
+                row = 16 * ((t - half + 8 * j) % 16)
+                keep = keep_ref[9 * half + t]
+                m_ref[row : row + 16, out_lanes] = part[:, lanes] * keep
+                m_ref[256 + row : 256 + row + 16, out_lanes] = turned[:, lanes] * keep
 
 
 def apply_dense(left, right, m_ref):
@@ -198,6 +203,7 @@
     y_ref,
     mask_ref,
     g_ref,
+    keep_ref,
     m_ref,
     rot_in,
     band,
@@ -249,6 +255,7 @@
         pl.semaphore_signal(barrier, inc=1, device_id=other, device_id_type=MESH)
 
     init_masks(mask_ref)
+    init_keep(keep_ref)
     m_ref[...] = jnp.zeros_like(m_ref)
     finish(loads)
 
@@ -286,11 +293,7 @@
             return remote(SWAP + g, band.at[step, 1 - core, group], r1.at[step, group], partner)
 
         def theirs(g, carry):
-            def body(h, carry):
-                gram_pairs(1 - core, [(ahead(x, g), 2 * h), (ahead(x, g), 2 * h + 1)])
-                return carry
-
-            lax.fori_loop(0, 2, body, 0)
+            gram_pairs(1 - core, [(ahead(x, g), j) for j in range(4)])
             if step == 0:
 
                 @pl.when(g == 0)
@@ -317,29 +320,19 @@
         def ours(g, carry):
             i = ahead(x, g)
 
-            def body(h2, carry):
-                gram_pairs(core, [(i, ahead(y, 2 * h2)), (i, ahead(y, 2 * h2 + 1))])
-
-                @pl.when(h2 == 0)
+            gram_pairs(core, [(i, ahead(y, h)) for h in range(4)])
+            swap(g).wait()
+            for h in range(4):
+                j = ahead(y, h)
+                acc1[i, j] = band[step, core, i, j] + r1[step, i, j]
+
+                @pl.when(g < 3)
                 def _():
-                    swap(g).wait()
-
-                for k in range(2):
-                    h = 2 * h2 + k
-                    j = ahead(y, h)
-                    acc1[i, j] = band[step, core, i, j] + r1[step, i, j]
-
-                    @pl.when(g < 3)
-                    def _():
-                        top(g, h).start()
-
-                    @pl.when(h < 3)
-                    def _():
-                        low(g, h).start()
-
-                return carry
-
-            return lax.fori_loop(0, 2, body, carry)
+                    top(g, h).start()
+
+                if h < 3:
+                    low(g, h).start()
+            return carry
 
         lax.fori_loop(0, 4, ours, 0)
 
@@ -405,15 +398,15 @@
         def apply_pair(side, i, k):
             sx, sy = source(i)
             p = side * half + 4 * sx + sy
-            build_dense(rot[side, sx, sy], m_ref.at[k])
+            build_dense(rot[side, sx, sy], keep_ref, m_ref.at[k])
             left = x_ref[hold[2 * p]]
             right = x_ref[hold[2 * p + 1]]
             cols = pl.ds(pl.multiple_of(p * 2 * BW, 2 * BW), 2 * BW)
             y_ref[:, cols] = apply_dense(left, right, m_ref.at[k])
 
         def first_half(h, carry):
-            for k in range(2):
-                i = 2 * h + k
+            for k in range(4):
+                i = 4 * h + k
 
                 @pl.when(i > 0)
                 def _():
@@ -421,20 +414,20 @@
                     forward(i).start()
 
             if step == 0:
-                for k in range(2):
-                    apply_pair(core, 2 * h + k, k)
+                for k in range(4):
+                    apply_pair(core, 4 * h + k, k)
             return carry
 
         def second_half(h, carry):
-            for k in range(2):
-                forwarded(2 * h + k).wait_recv()
+            for k in range(4):
+                forwarded(4 * h + k).wait_recv()
             if step == 0:
-                for k in range(2):
-                    apply_pair(1 - core, 2 * h + k, k)
+                for k in range(4):
+                    apply_pair(1 - core, 4 * h + k, k)
             return carry
 
-        lax.fori_loop(0, 8, first_half, 0)
-        lax.fori_loop(0, 8, second_half, 0)
+        lax.fori_loop(0, 4, first_half, 0)
+        lax.fori_loop(0, 4, second_half, 0)
         for i in range(1, 16):
             spread_out(i).wait_send()
         for i in range(16):
@@ -460,8 +453,9 @@
             pltpu.VMEM((2 * pairs, rows, BW), BF16),
             pltpu.VMEM((rows, cols), BF16),
             pltpu.VMEM((35, 8, 128), F32),
-            pltpu.VMEM((2, 3, BW, BW), F32),
-            pltpu.VMEM((2, 2 * BW, 2 * BW), BF16),
+            pltpu.VMEM((4, 3, BW, BW), F32),
+            pltpu.VMEM((18, 16, 128), BF16),
+            pltpu.VMEM((4, 2 * BW, 2 * BW), BF16),
             pltpu.VMEM((2, 4, 4, 32, BW), BF16),
             pltpu.VMEM((2, 2, 4, 4, 32, BW), F32),
             pltpu.VMEM((2, 4, 4, 32, BW), F32),
@@ -484,7 +478,9 @@
     return out, rot.reshape(pairs, 32, BW)
 
 
-def last_kernel(pairs, hold, y_hbm, rot, out_hbm, y_ref, m_ref, z_ref, load_sem, store_sem):
+def last_kernel(
+    pairs, hold, y_hbm, rot, out_hbm, y_ref, keep_ref, m_ref, z_ref, load_sem, store_sem
+):
     width = y_ref.shape[1] // CHUNKS
     per_chunk = pairs // CHUNKS
 
@@ -499,6 +495,7 @@
 
     for k in range(CHUNKS):
         load(k).start()
+    init_keep(keep_ref)
     m_ref[...] = jnp.zeros_like(m_ref)
     load(0).wait()
 
@@ -508,9 +505,9 @@
             load(i + 1).wait()
 
         def inner(h, carry):
-            for k in range(2):
-                q = i * per_chunk + 2 * h + k
-                build_dense(rot[q], m_ref.at[k])
+            for k in range(4):
+                q = i * per_chunk + 4 * h + k
+                build_dense(rot[q], keep_ref, m_ref.at[k])
                 a, b = seats_before(q, pairs)
                 cols = pl.ds(pl.multiple_of(q * 2 * BW, 2 * BW), 2 * BW)
                 z_ref[:, cols] = apply_dense(y_ref[:, block(a)], y_ref[:, block(b)], m_ref.at[k])
@@ -518,7 +515,7 @@
                 store(2 * q + 1).start()
             return carry
 
-        return lax.fori_loop(0, per_chunk // 2, inner, carry)
+        return lax.fori_loop(0, per_chunk // 4, inner, carry)
 
     lax.fori_loop(0, CHUNKS, body, 0)
 
@@ -540,7 +537,8 @@
         out_specs=hbm,
         scratch_shapes=[
             pltpu.VMEM((rows, cols), BF16),
-            pltpu.VMEM((2, 2 * BW, 2 * BW), BF16),
+            pltpu.VMEM((18, 16, 128), BF16),
+            pltpu.VMEM((4, 2 * BW, 2 * BW), BF16),
             pltpu.VMEM((rows, cols), BF16),
             pltpu.SemaphoreType.DMA((CHUNKS,)),
             pltpu.SemaphoreType.DMA((2 * pairs,)),

time: 92.3 us -> 88 us (0.953)
  Pallas kernels: 89.4 us -> 85.2 us
    pallas_call x1, Pallas kernels: 79.4 us -> 77 us  [main_call(): pl.pallas_call(functools.partial(main_kernel, pairs), out_shape=(jax.Shap...]
    pallas_call x1, Pallas kernels: 10.1 us -> 8.22 us  [last_call(): pl.pallas_call(functools.partial(last_kernel, pairs), out_shape=jax.Shape...]
where the time goes in v4:
time: 88 us; the launch traced here: 87.9 us
  Pallas kernels  85.2 us (97%)
  other arithmetic  2.67 us (3%)
    pallas_call x1, Pallas kernels, main_call(): pl.pallas_call(functools.partial(main_kernel, pairs), out_shape=(jax.Shap...  77 us
    pallas_call x1, Pallas kernels, last_call(): pl.pallas_call(functools.partial(last_kernel, pairs), out_shape=jax.Shape...  8.22 us
    reduce_sum x2, other arithmetic, occupants(): jnp.sum(jnp.where(matches, block_ids[None, :], 0), axis=1).astype(jnp.int32)  1.99 us

profile of v4, /device:TPU:1, one launch (start us, length us, event | category | flops | bytes accessed | tf_op | source)
XLA Modules:
  0.0 87.9 jit_solution(11154653514776277495)
XLA Ops:
  0.0 1.3 %select_reduce_fusion.hold = s32[64]{0:T(128)} fusion(s32[64]{0:T(128)} %param.3), kind=kLoop, calls=%fused_computation | loop fusion | flops 12224 | bytes 512 | tf_op jit(solution)/shard_map/reduce_sum | solution.py:29
  1.3 0.7 compare_select_fusion.2
  2.0 0.7 select_reduce_fusion.1.hold
  2.7 77.0 %shard_map.28 = (bf16[160,16384]{1,0:T(8,128)(2,1)}, bf16[2,4,4,32,256]{4,3,2,1,0:T(8,128)(2,1)}) custom-call(s32[64]{0:T(128)} %select_reduce_fusion.hold, bf16[160,16384]{1,0:T(8,128)(2,1)} %x_hbm.1), custom_call_target="tpu_custom_call" | custom-call | tf_op jit(solution)/shard_map/pallas_call | solution.py:444
  79.7 8.2 %shard_map.29 = bf16[160,16384]{1,0:T(8,128)(2,1)} custom-call(s32[64]{0:T(128)} %select_reduce_fusion.1.hold, bf16[160,16384]{1,0:T(8,128)(2,1)} %get-tuple-element.7.y_hbm, bf16[32,32,256]{2,1,0:T(8,128)(2,1)} %bitcast.1), custom_call_target="tpu_custom_call" | custom-call | tf_op jit(solution)/shard_map/pallas_call | solution.py:533

commit v5 on v4

--- a/solution.py
+++ b/solution.py
@@ -11,16 +11,6 @@
 BW = 256
 F32 = jnp.float32
 BF16 = jnp.bfloat16
-
-
-def advance(seat_of, total_slots):
-    pair_count = total_slots // 2
-    cycle_pos = jnp.where(seat_of % 2 == 0, seat_of // 2 - 1, total_slots - 2 - (seat_of - 1) // 2)
-    next_pos = (cycle_pos + 1) % (total_slots - 1)
-    new_slot = jnp.where(
-        next_pos < pair_count - 1, 2 * (next_pos + 1), 2 * (total_slots - 2 - next_pos) + 1
-    )
-    return jnp.where(seat_of == 0, 0, new_slot)
 
 
 def occupants(seat_of, total_slots):
@@ -488,9 +478,9 @@
         cols = pl.ds(pl.multiple_of(k * width, width), width)
         return pltpu.make_async_copy(y_hbm.at[:, cols], y_ref.at[:, cols], load_sem.at[k])
 
-    def store(seat):
+    def store(seat, before):
         return pltpu.make_async_copy(
-            z_ref.at[:, block(seat)], out_hbm.at[:, block(hold[seat])], store_sem.at[seat]
+            z_ref.at[:, block(seat)], out_hbm.at[:, block(hold[before])], store_sem.at[seat]
         )
 
     for k in range(CHUNKS):
@@ -511,19 +501,21 @@
                 a, b = seats_before(q, pairs)
                 cols = pl.ds(pl.multiple_of(q * 2 * BW, 2 * BW), 2 * BW)
                 z_ref[:, cols] = apply_dense(y_ref[:, block(a)], y_ref[:, block(b)], m_ref.at[k])
-                store(2 * q).start()
-                store(2 * q + 1).start()
+                store(2 * q, a).start()
+                store(2 * q + 1, b).start()
             return carry
 
         return lax.fori_loop(0, per_chunk // 4, inner, carry)
 
     lax.fori_loop(0, CHUNKS, body, 0)
 
-    def drain(seat, carry):
-        store(seat).wait()
+    def drain(q, carry):
+        a, b = seats_before(q, pairs)
+        store(2 * q, a).wait()
+        store(2 * q + 1, b).wait()
         return carry
 
-    lax.fori_loop(0, 2 * pairs, drain, 0)
+    lax.fori_loop(0, pairs, drain, 0)
 
 
 def last_call(y, holders, rot, pairs):
@@ -550,10 +542,9 @@
     slots = gradient.shape[1] // BW
     pairs = slots // 2
     seat_of = seating.astype(jnp.int32)
-    first = occupants(seat_of, slots)
-    second = occupants(advance(seat_of, slots), slots)
-    moved, rot = main_call(gradient, first, pairs)
-    return last_call(moved, second, rot, pairs)
+    holders = occupants(seat_of, slots)
+    moved, rot = main_call(gradient, holders, pairs)
+    return last_call(moved, holders, rot, pairs)
 
 
 def solution(mesh):

time: 88 us -> 86.7 us (0.985)
  other arithmetic: 2.67 us -> 1.36 us
    reduce_sum x2 -> x1, other arithmetic: 1.99 us -> 1.36 us  [occupants(): jnp.sum(jnp.where(matches, block_ids[None, :], 0), axis=1).astype(jnp.int32)]
where the time goes in v5:
time: 86.7 us; the launch traced here: 86.6 us
  Pallas kernels  85.2 us (98%)
  other arithmetic  1.36 us (2%)
    pallas_call x1, Pallas kernels, main_call(): pl.pallas_call(functools.partial(main_kernel, pairs), out_shape=(jax.Shap...  76.9 us
    pallas_call x1, Pallas kernels, last_call(): pl.pallas_call(functools.partial(last_kernel, pairs), out_shape=jax.Shape...  8.27 us

profile of v5, /device:TPU:1, one launch (start us, length us, event | category | flops | bytes accessed | tf_op | source)
XLA Modules:
  0.0 86.6 jit_solution(9044378103150699374)
XLA Ops:
  0.0 1.4 %select_reduce_fusion.hold = s32[64]{0:T(128)} fusion(s32[64]{0:T(128)} %param.3), kind=kLoop, calls=%fused_computation | loop fusion | flops 12224 | bytes 512 | tf_op jit(solution)/shard_map/reduce_sum | solution.py:19
  1.4 76.9 %shard_map.28 = (bf16[160,16384]{1,0:T(8,128)(2,1)}, bf16[2,4,4,32,256]{4,3,2,1,0:T(8,128)(2,1)}) custom-call(s32[64]{0:T(128)} %select_reduce_fusion.hold, bf16[160,16384]{1,0:T(8,128)(2,1)} %x_hbm.1), custom_call_target="tpu_custom_call" | custom-call | tf_op jit(solution)/shard_map/pallas_call | solution.py:434
  78.3 8.3 %shard_map.29 = bf16[160,16384]{1,0:T(8,128)(2,1)} custom-call(s32[64]{0:T(128)} %select_reduce_fusion.hold, bf16[160,16384]{1,0:T(8,128)(2,1)} %get-tuple-element.7.y_hbm, bf16[32,32,256]{2,1,0:T(8,128)(2,1)} %bitcast.1), custom_call_target="tpu_custom_call" | custom-call | tf_op jit(solution)/shard_map/pallas_call | solution.py:525

commit v6 on v5

--- a/solution.py
+++ b/solution.py
@@ -283,17 +283,18 @@
             return remote(SWAP + g, band.at[step, 1 - core, group], r1.at[step, group], partner)
 
         def theirs(g, carry):
-            gram_pairs(1 - core, [(ahead(x, g), j) for j in range(4)])
+            gram_pairs(1 - core, [(ahead(x, 2 * g + k), j) for k in range(2) for j in range(4)])
             if step == 0:
 
                 @pl.when(g == 0)
                 def _():
                     pl.semaphore_wait(barrier, len(greeted))
 
-            swap(g).start()
+            swap(2 * g).start()
+            swap(2 * g + 1).start()
             return carry
 
-        lax.fori_loop(0, 4, theirs, 0)
+        lax.fori_loop(0, 2, theirs, 0)
 
         def top(g, h):
             i, j = ahead(x, g), ahead(y, h)
@@ -443,7 +444,7 @@
             pltpu.VMEM((2 * pairs, rows, BW), BF16),
             pltpu.VMEM((rows, cols), BF16),
             pltpu.VMEM((35, 8, 128), F32),
-            pltpu.VMEM((4, 3, BW, BW), F32),
+            pltpu.VMEM((8, 3, BW, BW), F32),
             pltpu.VMEM((18, 16, 128), BF16),
             pltpu.VMEM((4, 2 * BW, 2 * BW), BF16),
             pltpu.VMEM((2, 4, 4, 32, BW), BF16),

time: 86.7 us -> 85.6 us (0.987)
  Pallas kernels: 85.2 us -> 84.1 us
    pallas_call x1, Pallas kernels: 76.9 us -> 75.8 us  [main_call(): pl.pallas_call(functools.partial(main_kernel, pairs), out_shape=(jax.Shap...]
where the time goes in v6:
time: 85.6 us; the launch traced here: 85.5 us
  Pallas kernels  84.1 us (98%)
  other arithmetic  1.36 us (2%)
    pallas_call x1, Pallas kernels, main_call(): pl.pallas_call(functools.partial(main_kernel, pairs), out_shape=(jax.Shap...  75.8 us
    pallas_call x1, Pallas kernels, last_call(): pl.pallas_call(functools.partial(last_kernel, pairs), out_shape=jax.Shape...  8.29 us

profile of v6, /device:TPU:1, one launch (start us, length us, event | category | flops | bytes accessed | tf_op | source)
XLA Modules:
  0.0 85.5 jit_solution(13379679938601356277)
XLA Ops:
  0.0 1.4 %select_reduce_fusion.hold = s32[64]{0:T(128)} fusion(s32[64]{0:T(128)} %param.3), kind=kLoop, calls=%fused_computation | loop fusion | flops 12224 | bytes 512 | tf_op jit(solution)/shard_map/reduce_sum | solution.py:19
  1.4 75.8 %shard_map.28 = (bf16[160,16384]{1,0:T(8,128)(2,1)}, bf16[2,4,4,32,256]{4,3,2,1,0:T(8,128)(2,1)}) custom-call(s32[64]{0:T(128)} %select_reduce_fusion.hold, bf16[160,16384]{1,0:T(8,128)(2,1)} %x_hbm.1), custom_call_target="tpu_custom_call" | custom-call | tf_op jit(solution)/shard_map/pallas_call | solution.py:435
  77.2 8.3 %shard_map.29 = bf16[160,16384]{1,0:T(8,128)(2,1)} custom-call(s32[64]{0:T(128)} %select_reduce_fusion.hold, bf16[160,16384]{1,0:T(8,128)(2,1)} %get-tuple-element.7.y_hbm, bf16[32,32,256]{2,1,0:T(8,128)(2,1)} %bitcast.1), custom_call_target="tpu_custom_call" | custom-call | tf_op jit(solution)/shard_map/pallas_call | solution.py:526
